TPU v7x, 32 devices: a whole 2x2x4 slice. The times are simulated.
32 devices in a mesh: orb: 2 (over x), grid: 16 (over z, y, core).
Axes of the slice: x: 2, y: 2, z: 4, core: 2. Of those that a mesh axis runs over, the one named last changes fastest.
Arguments:
- orbitals: bfloat16 [2, 1024, 2304], P('orb', 'grid'), may hold values from -6 to 6
- continuum: bfloat16 [4, 1024, 2304], P(None, 'grid'), may hold values from -6 to 6
- harmonic_table: bfloat16 [2560, 2304], P('orb'), may hold values from -0.125 to 0.125
- ang_weight: float32 [2560], P('orb'), may hold values from 0.5 to 2
- channel_lm: int32 [2304], replicated, may hold values from 0 to 2303, each once
Outputs:
- exchange_out: float32 [2304, 4, 1024], P('orb', None, 'grid')
Inputs may be any that keep to these rules, and one draw needn't show every extreme that they name: channel_lm names each harmonic index lm = l * l + l + m (l up to 47) exactly once.
All inputs are finite; a program needn't handle non-finite values.
Results may differ from a plain program's by a relative error of at most 0.03.
Values may be sent and summed in bfloat16 or wider, within the bound.
No kernel may reach another device: no remote copies, remote signals or barrier semaphores. Data moves between devices by JAX's collectives and lax.ppermute only.
A program may use at most 128 MiB of HBM per device.

v0:
```python
import math
import jax
import jax.numpy as jnp
from jax import lax
from jax.sharding import PartitionSpec as P

LMAX = 47
LM = 2304
LOG_SPAN = 7.0


def combine(earlier, later):
    return (earlier[0] * later[0], earlier[1] * later[0] + later[1])


def channel_degree(lm_index):
    levels = jnp.arange(1, LMAX + 1, dtype=jnp.int32)
    return jnp.sum((lm_index[:, None] >= levels * levels).astype(jnp.float32), axis=1)


def line_sums(forward_source, backward_source, decay_rate, block_size):
    lead_first, lead_second, count, channels = forward_source.shape
    block_count = count // block_size
    forward_blocks = forward_source.reshape(
        lead_first, lead_second, block_count, block_size, channels
    )
    backward_blocks = backward_source.reshape(
        lead_first, lead_second, block_count, block_size, channels
    )
    forward = forward_blocks
    backward = backward_blocks
    for distance in range(1, block_size):
        factor = jnp.exp(-decay_rate * distance)
        padding = jnp.zeros((lead_first, lead_second, block_count, distance, channels), jnp.float32)
        forward = forward + factor * jnp.concatenate(
            [padding, forward_blocks[:, :, :, : block_size - distance]], axis=3
        )
        backward = backward + factor * jnp.concatenate(
            [backward_blocks[:, :, :, distance:], padding], axis=3
        )
    block_decay = jnp.broadcast_to(
        jnp.exp(-decay_rate * block_size), (lead_first, lead_second, block_count, channels)
    )
    forward_total = lax.associative_scan(
        combine, (block_decay, forward[:, :, :, block_size - 1]), axis=2
    )[1]
    backward_total = lax.associative_scan(
        combine, (block_decay, backward[:, :, :, 0]), reverse=True, axis=2
    )[1]
    boundary = jnp.zeros((lead_first, lead_second, 1, channels), jnp.float32)
    earlier_sum = jnp.concatenate([boundary, forward_total[:, :, : block_count - 1]], axis=2)
    later_sum = jnp.concatenate([backward_total[:, :, 1:], boundary], axis=2)
    offsets = jnp.arange(block_size, dtype=jnp.float32)[:, None]
    forward = forward + jnp.exp(-decay_rate * (offsets + 1.0)) * earlier_sum[:, :, :, None, :]
    backward = (
        backward + jnp.exp(-decay_rate * (block_size - offsets)) * later_sum[:, :, :, None, :]
    )
    shape = forward_source.shape
    return (
        forward.reshape(shape),
        backward.reshape(shape),
        forward_total[:, :, block_count - 1],
        backward_total[:, :, 0],
    )


def local_lines(density, degree, points):
    count = density.shape[2]
    increment = LOG_SPAN / points
    positions = jnp.arange(count, dtype=jnp.int32).astype(jnp.float32)[:, None]
    radius = jnp.exp((positions + 1.0 - points) * increment)
    decay_rate = degree * increment
    source = increment * radius * density
    scaled = increment * density
    forward, backward, forward_end, backward_end = line_sums(
        source, scaled, decay_rate, math.gcd(count, 16)
    )
    return (forward, backward, forward_end, backward_end, radius, scaled, decay_rate)


def finish_potential(forward, backward, radius, scaled, degree):
    factor = 4.0 / (2.0 * degree + 1.0)
    return factor * (forward / radius + backward - scaled)


def shards(orbitals, continuum, harmonic_table, ang_weight, channel_lm):
    analysis = (ang_weight[:, None] * harmonic_table.astype(jnp.float32)).astype(jnp.bfloat16)
    phi_ang = jnp.einsum(
        "al,irl->ira",
        harmonic_table,
        lax.all_gather(orbitals, "orb", axis=0, tiled=True),
        preferred_element_type=jnp.float32,
    ).astype(jnp.bfloat16)
    continuum_angular = jnp.einsum(
        "al,krl->kra", harmonic_table, continuum, preferred_element_type=jnp.float32
    ).astype(jnp.bfloat16)
    pair_values = (
        phi_ang.astype(jnp.float32)[:, None] * continuum_angular.astype(jnp.float32)[None]
    ).astype(jnp.bfloat16)
    density = lax.psum_scatter(
        jnp.einsum(
            "al,ikra->ikrl", analysis, pair_values, preferred_element_type=jnp.float32
        ).astype(jnp.bfloat16),
        "orb",
        scatter_dimension=0,
        tiled=True,
    )
    local_count = LM // lax.axis_size("grid")
    local_channel_index = lax.dynamic_slice_in_dim(
        channel_lm, lax.axis_index("grid") * local_count, local_count
    )
    degree = channel_degree(local_channel_index)
    line_density = lax.all_to_all(density, "grid", split_axis=3, concat_axis=2, tiled=True)
    points = line_density.shape[2]
    forward, backward, forward_end, backward_end, radius, scaled, decay_rate = local_lines(
        line_density.astype(jnp.float32), degree, points
    )
    potential = finish_potential(forward, backward, radius, scaled, degree).astype(jnp.bfloat16)
    radial_potential = lax.all_to_all(potential, "grid", split_axis=2, concat_axis=3, tiled=True)
    pot_ang = jnp.einsum(
        "al,ikrl->ikra",
        harmonic_table,
        lax.all_gather(radial_potential, "orb", axis=0, tiled=True),
        preferred_element_type=jnp.float32,
    )
    weighted_values = jnp.sum(phi_ang.astype(jnp.float32)[:, None] * pot_ang, axis=0)
    product = weighted_values.astype(jnp.bfloat16)
    return -lax.psum_scatter(
        jnp.einsum("al,kra->lkr", analysis, product, preferred_element_type=jnp.float32),
        "orb",
        scatter_dimension=0,
        tiled=True,
    )


def solution(mesh):
    return jax.shard_map(
        shards,
        mesh=mesh,
        in_specs=(P("orb", "grid", None), P(None, "grid", None), P("orb", None), P("orb"), P()),
        out_specs=P("orb", None, "grid"),
        check_vma=False,
    )
```

profile of v0, /device:TPU:0, one launch (start us, length us, event | category | flops | bytes accessed | tf_op | source)
XLA Modules:
  0.0 537.0 jit_solution(362612435213121791)
XLA Ops:
  6.5 11.0 %all_gather.6 = bf16[2,64,2304]{2,1,0:T(8,128)(2,1)S(1)} all-gather(bf16[1,64,2304]{2,1,0:T(8,128)(2,1)} %param.5), channel_id=1, replica_groups=mesh['orb'=2,'grid'=16] {'orb'}, dimensions={0}, use_global_device_ids=true | all-gather | bytes 884736 | tf_op jit(solution)/shard_map/all_gather | solution.py:91
  17.5 4.8 fusion.27
  24.1 5.0 fusion.10
  29.2 36.4 %reduce-scatter.3.cloned.1.call-done = bf16[1,4,64,2304]{3,2,1,0:T(8,128)(2,1)} async-done(((bf16[2,4,64,2304]{3,2,1,0:T(8,128)(2,1)}), bf16[1,4,64,2304]{3,2,1,0:T(8,128)(2,1)}) %reduce-scatter.3.cloned.1.call-update) | async-done | bytes 1179664 | tf_op jit(solution)/shard_map/reduce_scatter | solution.py:100
  72.2 5.6 %all-to-all-start = ((bf16[16,2,18432]{2,1,0:T(2,128)(2,1)}), bf16[16,2,18432]{2,1,0:T(2,128)(2,1)S(1)}, u32[]{:S(2)}, u32[]{:S(2)}) async-start(bf16[16,2,18432]{2,1,0:T(2,128)(2,1)} %reshape.319), calls=%async_computation.1 | async-start | bytes 2359296 | tf_op jit(solution)/shard_map/all_to_all | solution.py:113
  81.4 21.5 %all-to-all-done = bf16[16,2,18432]{2,1,0:T(2,128)(2,1)S(1)} async-done(((bf16[16,2,18432]{2,1,0:T(2,128)(2,1)}), bf16[16,2,18432]{2,1,0:T(2,128)(2,1)S(1)}, u32[]{:S(2)}, u32[]{:S(2)}) %all-to-all-start) | async-done | bytes 1179680 | tf_op jit(solution)/shard_map/all_to_all | solution.py:113
  104.5 5.4 %copy.132 = f32[1,4,64,16,144]{4,2,3,1,0:T(8,128)} copy(bf16[1,4,64,16,144]{2,1,4,3,0:T(4,128)(2,1)S(1)} %bitcast.77) | data formatting | bytes 3538944 | tf_op jit(solution)/shard_map/convert_element_type | solution.py:116
  109.8 7.8 %copy_multiply_fusion = f32[1,4,64,16,144]{4,0,3,2,1:T(1,128)S(1)} fusion(f32[1,4,64,16,144]{4,3,2,1,0:T(8,128)} %bitcast.74, f32[64,16]{1,0:T(8,128)S(1)} %copy-done.29), kind=kLoop, calls=%fused_computation.17 | loop fusion | flops 589824 | bytes 4722688 | tf_op jit(solution)/shard_map/mul | solution.py:73
  117.7 5.5 %slice.492 = f32[1,4,64,15,144]{4,0,3,2,1:T(1,128)} slice(f32[1,4,64,16,144]{4,0,3,2,1:T(1,128)S(1)} %copy_multiply_fusion), slice={[0:1], [0:4], [0:64], [0:15], [0:144]} | slice | bytes 4423680 | tf_op jit(solution)/shard_map/slice | solution.py:36
  123.1 5.2 slice.493
  154.5 43.8 %multiply_add_fusion.3 = f32[1,4,64,16,144]{4,0,3,2,1:T(1,128)S(1)} fusion(f32[1,4,64,1,144]{4,0,3,2,1:T(1,128)S(1)} %slice.506, f32[1,4,64,2,144]{4,0,3,2,1:T(1,128)S(1)} %slice.505, f32[1,4,64,3,144]{4,0,3,2,1:T(1,128)S(1)} %slice.504, f32[1,4,64,4,144]{4,0,3,2,1:T(1,128)S(1)} %slice.503, f32[1,4,64,5,144]{4,0,3,2,1:T(1,128)} %slice.502, ...), kind=kLoop, calls=%fused_computation.21 | loop fusion | flops 18284544 | bytes 22426048 | tf_op jit(solution)/shard_map/add | solution.py:35
  235.9 8.1 %copy.157 = f32[1,4,64,15,144]{4,0,3,2,1:T(1,128)} copy(f32[1,4,64,15,144]{4,3,2,1,0:T(8,128)} %slice.526) | data formatting | bytes 4423680
  244.0 8.1 %copy.156 = f32[1,4,64,14,144]{4,0,3,2,1:T(1,128)} copy(f32[1,4,64,14,144]{4,3,2,1,0:T(8,128)} %slice.527) | data formatting | bytes 4128768
  252.2 5.4 %copy.155 = f32[1,4,64,13,144]{4,0,3,2,1:T(1,128)} copy(f32[1,4,64,13,144]{4,3,2,1,0:T(8,128)S(1)} %copy-done.10) | data formatting | bytes 3833856
  273.2 4.8 copy.149
  288.4 35.6 %multiply_add_fusion.1 = f32[1,4,64,16,144]{4,0,3,2,1:T(1,128)S(1)} fusion(f32[1,4,64,2,144]{4,0,3,2,1:T(1,128)S(1)} %copy.144, f32[1,4,64,3,144]{4,0,3,2,1:T(1,128)S(1)} %copy.145, f32[1,4,64,4,144]{4,0,3,2,1:T(1,128)S(1)} %copy.146, f32[1,4,64,5,144]{4,0,3,2,1:T(1,128)S(1)} %copy.147, f32[1,4,64,6,144]{4,0,3,2,1:T(1,128)} %copy.148, ...), kind=kLoop, calls=%fused_computation.19 | loop fusion | flops 16515072 | bytes 22273920 | tf_op jit(solution)/shard_map/add | solution.py:38
  331.0 10.6 %pad.124 = f32[1,4,16,144]{3,0,2,1:T(1,128)S(1)} pad(f32[1,4,8,144]{3,0,2,1:T(1,128)} %pad_maximum_fusion.5, f32[]{:T(128)} %constant.31.clone.1), padding=0_0_0x0_0_0x0_1_1x0_0_0 | pad | bytes 55300 | tf_op jit(solution)/shard_map/pad | solution.py:47
  349.5 9.2 %multiply_add_fusion.2 = f32[1,4,64,16,144]{4,0,3,2,1:T(1,128)} fusion(f32[1,4,64,16,144]{4,0,3,2,1:T(1,128)} %copy-done.6, f32[4,64,144]{2,1,0:T(8,128)S(1)} %pad_bitcast_fusion.1, f32[16,144]{1,0:T(8,128)S(1)} %copy-done.31), kind=kLoop, calls=%fused_computation.20 | loop fusion | flops 1179648 | bytes 4875264 | tf_op jit(solution)/shard_map/add | solution.py:54
  369.5 7.0 %copy.134 = f32[1,4,64,16,144]{4,2,3,1,0:T(8,128)} copy(f32[1,4,64,16,144]{2,1,4,3,0:T(4,128)} %bitcast.78) | data formatting | bytes 4718592 | tf_op jit(solution)/shard_map/mul | solution.py:74
  384.5 54.8 %all_to_all.27 = bf16[1,4,1024,144]{3,1,0,2:T(4,128)(2,1)S(1)} all-to-all(bf16[1,4,1024,144]{3,1,0,2:T(4,128)(2,1)S(1)} %copy.127), channel_id=1, replica_groups=mesh['orb'=2,'grid'=16] {'grid'}, dimensions={2} | all-to-all | bytes 2359296 | tf_op jit(solution)/shard_map/all_to_all | solution.py:119
  444.6 35.6 %all-gather.2.cloned.1.call-done = bf16[2,4,64,2304]{3,2,1,0:T(8,128)(2,1)} async-done(((bf16[1,4,64,2304]{3,2,1,0:T(8,128)(2,1)}), bf16[2,4,64,2304]{3,2,1,0:T(8,128)(2,1)}) %all-gather.2.cloned.1.call-update) | async-done | bytes 2359312 | tf_op jit(solution)/shard_map/all_gather | solution.py:123
  480.3 6.7 %fusion.30 = bf16[4,64,1280]{2,1,0:T(8,128)(2,1)S(1)} fusion(bf16[2,4,64,2304]{3,2,1,0:T(8,128)(2,1)} %all-gather.2.cloned.1.call-done, bf16[1280,2304]{1,0:T(8,128)(2,1)} %param.7, f32[2,64,1280]{2,1,0:T(8,128)S(1)} %copy-done.27), kind=kOutput, calls=%fused_computation.31 | convolution fusion | flops 3020881920 | bytes 9568256 | tf_op jit(solution)/shard_map/al,ikrl->ikra/dot_general | solution.py:120
  487.0 6.0 %fusion.8 = f32[2304,4,64]{0,2,1:T(8,128)} fusion(bf16[1280,2304]{1,0:T(8,128)(2,1)} %param.7, f32[1280]{0:T(1024)S(1)} %copy-done.75, bf16[4,64,1280]{2,1,0:T(8,128)(2,1)S(1)} %fusion.30), kind=kOutput, calls=%fused_computation.9 | convolution fusion | flops 1518796800 | bytes 8918016 | tf_op jit(solution)/shard_map/al,kra->lkr/dot_general | solution.py:129
  493.0 34.9 %reduce-scatter.5.cloned.1.call-done = f32[1152,4,64]{0,2,1:T(8,128)} async-done(((f32[2304,4,64]{0,2,1:T(8,128)}), f32[1152,4,64]{0,2,1:T(8,128)}) %reduce-scatter.5.cloned.1.call-update) | async-done | bytes 1179664 | tf_op jit(solution)/shard_map/reduce_scatter | solution.py:128
  (309 shorter events, 143.1 us)
Async XLA Ops:
  6.5 15.8 %copy-start = (bf16[4,64,2304]{2,1,0:T(8,128)(2,1)S(1)}, bf16[4,64,2304]{2,1,0:T(8,128)(2,1)}, u32[]{:S(2)}) copy-start(bf16[4,64,2304]{2,1,0:T(8,128)(2,1)} %param.6) | copy-start | bytes 3538948
  6.5 59.0 %reduce-scatter.3.cloned.1.call-start = ((), (), s32[]{:S(2)}) async-start(), calls=%async_computation.4 | async-start | bytes 3538944 | tf_op jit(solution)/shard_map/reduce_scatter | solution.py:100
  6.5 15.8 %slice-start.1 = ((s8[5898240]{0:T(1024)(128)(4,1)}), s8[4194304]{0:T(1024)(128)(4,1)S(1)}, s32[]{:S(2)}) async-start(s8[5898240]{0:T(1024)(128)(4,1)} %bitcast.80), calls=%async_computation.8 | async-start | bytes 8388608
  72.2 30.8 %all-to-all-start = ((bf16[16,2,18432]{2,1,0:T(2,128)(2,1)}), bf16[16,2,18432]{2,1,0:T(2,128)(2,1)S(1)}, u32[]{:S(2)}, u32[]{:S(2)}) async-start(bf16[16,2,18432]{2,1,0:T(2,128)(2,1)} %reshape.319), calls=%async_computation.1 | async-start | bytes 2359296 | tf_op jit(solution)/shard_map/all_to_all | solution.py:113
  77.8 402.5 %all-gather.2.cloned.1.call-start = ((), (), s32[]{:S(2)}) async-start(), calls=%async_computation.5 | async-start | bytes 3538944 | tf_op jit(solution)/shard_map/all_gather | solution.py:123
  154.4 46.2 %copy-start.32 = (f32[144]{0:T(256)S(1)}, f32[144]{0:T(256)}, u32[]{:S(2)}) copy-start(f32[144]{0:T(256)} %get-tuple-element.42) | copy-start | bytes 1732
  154.4 46.3 %copy-start.68 = (f32[144]{0:T(256)S(1)}, f32[144]{0:T(256)}, u32[]{:S(2)}) copy-start(f32[144]{0:T(256)} %get-tuple-element.43) | copy-start | bytes 1732
  154.4 46.4 %copy-start.69 = (f32[144]{0:T(256)S(1)}, f32[144]{0:T(256)}, u32[]{:S(2)}) copy-start(f32[144]{0:T(256)} %get-tuple-element.47) | copy-start | bytes 1732
  154.4 46.5 %copy-start.70 = (f32[144]{0:T(256)S(1)}, f32[144]{0:T(256)}, u32[]{:S(2)}) copy-start(f32[144]{0:T(256)} %get-tuple-element.46) | copy-start | bytes 1732
  154.4 46.5 %copy-start.71 = (f32[144]{0:T(256)S(1)}, f32[144]{0:T(256)}, u32[]{:S(2)}) copy-start(f32[144]{0:T(256)} %get-tuple-element.44) | copy-start | bytes 1732
  154.4 46.5 %copy-start.73 = (f32[144]{0:T(256)S(1)}, f32[144]{0:T(256)}, u32[]{:S(2)}) copy-start(f32[144]{0:T(256)} %get-tuple-element.45) | copy-start | bytes 1732
  208.7 26.2 %copy-start.2 = (f32[1,4,64,16,144]{4,3,2,1,0:T(8,128)}, f32[1,4,64,16,144]{4,3,2,1,0:T(8,128)S(1)}, u32[]{:S(2)}) copy-start(f32[1,4,64,16,144]{4,3,2,1,0:T(8,128)S(1)} %broadcast_multiply_fusion.1) | copy-start | bytes 7077892
  271.0 17.1 %copy-start.19 = (f32[1,4,64,11,144]{4,0,3,2,1:T(1,128)S(1)}, f32[1,4,64,11,144]{4,0,3,2,1:T(1,128)}, u32[]{:S(2)}) copy-start(f32[1,4,64,11,144]{4,0,3,2,1:T(1,128)} %copy.153) | copy-start | bytes 4866052
  273.2 14.4 %copy-start.23 = (f32[1,4,64,2,144]{4,3,2,1,0:T(2,128)S(1)}, f32[1,4,64,2,144]{4,3,2,1,0:T(2,128)}, u32[]{:S(2)}) copy-start(f32[1,4,64,2,144]{4,3,2,1,0:T(2,128)} %slice.539) | copy-start | bytes 884740
  273.2 15.0 %copy-start.18 = (f32[1,4,64,13,144]{4,0,3,2,1:T(1,128)S(1)}, f32[1,4,64,13,144]{4,0,3,2,1:T(1,128)}, u32[]{:S(2)}) copy-start(f32[1,4,64,13,144]{4,0,3,2,1:T(1,128)} %copy.155) | copy-start | bytes 5750788
  288.4 35.6 %copy-start.22 = (f32[1,4,64,1,144]{4,3,2,1,0:T(1,128)S(1)}, f32[1,4,64,1,144]{4,3,2,1,0:T(1,128)}, u32[]{:S(2)}) copy-start(f32[1,4,64,1,144]{4,3,2,1,0:T(1,128)} %slice.540) | copy-start | bytes 442372
  288.4 35.6 %copy-start.36 = (f32[144]{0:T(256)S(1)}, f32[144]{0:T(256)}, u32[]{:S(2)}) copy-start(f32[144]{0:T(256)} %get-tuple-element.41) | copy-start | bytes 1732
  326.3 19.3 %copy-start.24 = (f32[1,4,64,144]{3,0,2,1:T(1,128)}, f32[1,4,64,144]{3,0,2,1:T(1,128)S(1)}, u32[]{:S(2)}) copy-start(f32[1,4,64,144]{3,0,2,1:T(1,128)S(1)} %slice_bitcast_fusion) | copy-start | bytes 442372
  329.6 17.6 %slice-start.4 = ((f32[1,4,64,144]{3,0,2,1:T(1,128)}), f32[1,4,1,144]{3,0,2,1:T(1,128)S(1)}, s32[]{:S(2)}) async-start(f32[1,4,64,144]{3,0,2,1:T(1,128)} %copy-done.25), calls=%async_computation.11 | async-start | bytes 8192 | tf_op jit(solution)/shard_map/slice | solution.py:44
  329.6 17.6 %copy-start.28 = (f32[1,4,31,144]{3,0,2,1:T(1,128)S(1)}, f32[1,4,31,144]{3,0,2,1:T(1,128)}, u32[]{:S(2)}) copy-start(f32[1,4,31,144]{3,0,2,1:T(1,128)} %fusion.38) | copy-start | bytes 214276
  439.3 41.0 %copy-start.27 = (f32[2,64,1280]{2,1,0:T(8,128)S(1)}, f32[2,64,1280]{2,1,0:T(8,128)}, u32[]{:S(2)}) copy-start(f32[2,64,1280]{2,1,0:T(8,128)} %copy-done.26) | copy-start | bytes 1966084
  444.6 42.4 %copy-start.75 = (f32[1280]{0:T(1024)S(1)}, f32[1280]{0:T(1024)}, u32[]{:S(2)}) copy-start(f32[1280]{0:T(1024)} %param.8) | copy-start | bytes 15364
  444.6 83.3 %reduce-scatter.5.cloned.1.call-start = ((), (), s32[]{:S(2)}) async-start(), calls=%async_computation.6 | async-start | bytes 3538944 | tf_op jit(solution)/shard_map/reduce_scatter | solution.py:128
  487.0 43.3 %copy-start.1 = (bf16[4,64,2304]{2,1,0:T(8,128)(2,1)S(1)}, bf16[4,64,2304]{2,1,0:T(8,128)(2,1)}, u32[]{:S(2)}) copy-start(bf16[4,64,2304]{2,1,0:T(8,128)(2,1)} %param.6) | copy-start | bytes 3538948
  (61 other events, 344.4 us)
Sparse Core Ops, SparseCore 0:
  29.3 36.1 reduce-scatter.2
  444.7 35.5 all-gather.1
  493.1 34.6 reduce-scatter.4
where the time goes:
time: 543 us; the launch traced here: 537 us
  local copies, waits for them, and re-layouts  180 us (33%)
  waiting for transfers between devices  128 us (24%)
  other arithmetic  118 us (22%)
  blocking collectives  65.8 us (12%)
  matrix products  24.2 us (4%)
  between operations  14.9 us (3%)
  starting transfers between devices  5.71 us (1%)
    unnamed x179, local copies, waits for them, and re-layouts  69.2 us
    all_to_all x1, blocking collectives, shards(): lax.all_to_all(potential, 'grid', split_axis=2, concat_axis=3, tiled=True)  54.8 us
    add x1, other arithmetic, line_sums(): forward + factor * jnp.concatenate([padding, forward_blocks[:, :, :, :blo...  43.8 us
    reduce_scatter x1, waiting for transfers between devices, shards(): lax.psum_scatter(jnp.einsum('al,ikra->ikrl', analysis, pair_values, prefe...  36.4 us
    slice x15, local copies, waits for them, and re-layouts, line_sums(): forward_blocks[:, :, :, :block_size - distance]  36.3 us
    add x2, other arithmetic, line_sums(): backward + factor * jnp.concatenate([backward_blocks[:, :, :, distance:],...  36.2 us
    all_gather x1, waiting for transfers between devices, shards(): lax.all_gather(radial_potential, 'orb', axis=0, tiled=True)  35.6 us
    reduce_scatter x1, waiting for transfers between devices, shards(): lax.psum_scatter(jnp.einsum('al,kra->lkr', analysis, product, preferred_e...  34.9 us
  transfers between devices with their start and end apart: 4, of which 4 were waited for; matrix products, arithmetic and copies ran while one was open for 1% of the time, Pallas kernels for 0%

commit v1 on v0

--- a/solution.py
+++ b/solution.py
@@ -116,7 +116,12 @@
         line_density.astype(jnp.float32), degree, points
     )
     potential = finish_potential(forward, backward, radius, scaled, degree).astype(jnp.bfloat16)
-    radial_potential = lax.all_to_all(potential, "grid", split_axis=2, concat_axis=3, tiled=True)
+    radial_potential = jnp.concatenate(
+        lax.all_to_all(
+            jnp.stack(jnp.split(potential, lax.axis_size("grid"), axis=2)), "grid", 0, 0
+        ),
+        axis=3,
+    )
     pot_ang = jnp.einsum(
         "al,ikrl->ikra",
         harmonic_table,

time: 543 us -> 542 us (level)
    unnamed x179 -> x194, local copies, waits for them, and re-layouts: 69.2 us -> 69.4 us
where the time goes in v1:
time: 542 us; the launch traced here: 536 us
  local copies, waits for them, and re-layouts  178 us (33%)
  waiting for transfers between devices  128 us (24%)
  other arithmetic  118 us (22%)
  blocking collectives  65.8 us (12%)
  matrix products  24.2 us (4%)
  between operations  15 us (3%)
  starting transfers between devices  5.71 us (1%)
    unnamed x194, local copies, waits for them, and re-layouts  69.4 us
    all_to_all x1, blocking collectives, shards(): lax.all_to_all(jnp.stack(jnp.split(potential, lax.axis_size('grid'), axis...  54.8 us
    add x1, other arithmetic, line_sums(): forward + factor * jnp.concatenate([padding, forward_blocks[:, :, :, :blo...  43.8 us
    reduce_scatter x1, waiting for transfers between devices, shards(): lax.psum_scatter(jnp.einsum('al,ikra->ikrl', analysis, pair_values, prefe...  36.4 us
    slice x15, local copies, waits for them, and re-layouts, line_sums(): forward_blocks[:, :, :, :block_size - distance]  36.3 us
    add x2, other arithmetic, line_sums(): backward + factor * jnp.concatenate([backward_blocks[:, :, :, distance:],...  36.2 us
    all_gather x1, waiting for transfers between devices, shards(): lax.all_gather(radial_potential, 'orb', axis=0, tiled=True)  35.6 us
    reduce_scatter x1, waiting for transfers between devices, shards(): lax.psum_scatter(jnp.einsum('al,kra->lkr', analysis, product, preferred_e...  34.9 us
  transfers between devices with their start and end apart: 4, of which 4 were waited for; matrix products, arithmetic and copies ran while one was open for 1% of the time, Pallas kernels for 0%

profile of v1, /device:TPU:0, one launch (start us, length us, event | category | flops | bytes accessed | tf_op | source)
XLA Modules:
  0.0 535.7 jit_solution(16486263948692369538)
XLA Ops:
  6.5 11.0 %all_gather.6 = bf16[2,64,2304]{2,1,0:T(8,128)(2,1)S(1)} all-gather(bf16[1,64,2304]{2,1,0:T(8,128)(2,1)} %param.5), channel_id=1, replica_groups=mesh['orb'=2,'grid'=16] {'orb'}, dimensions={0}, use_global_device_ids=true | all-gather | bytes 884736 | tf_op jit(solution)/shard_map/all_gather | solution.py:91
  17.5 4.8 fusion.27
  24.1 5.0 fusion.10
  29.2 36.4 %reduce-scatter.3.cloned.1.call-done = bf16[1,4,64,2304]{3,2,1,0:T(8,128)(2,1)} async-done(((bf16[2,4,64,2304]{3,2,1,0:T(8,128)(2,1)}), bf16[1,4,64,2304]{3,2,1,0:T(8,128)(2,1)}) %reduce-scatter.3.cloned.1.call-update) | async-done | bytes 1179664 | tf_op jit(solution)/shard_map/reduce_scatter | solution.py:100
  72.2 5.6 %all-to-all-start = ((bf16[16,2,18432]{2,1,0:T(2,128)(2,1)}), bf16[16,2,18432]{2,1,0:T(2,128)(2,1)S(1)}, u32[]{:S(2)}, u32[]{:S(2)}) async-start(bf16[16,2,18432]{2,1,0:T(2,128)(2,1)} %reshape.327), calls=%async_computation.1 | async-start | bytes 2359296 | tf_op jit(solution)/shard_map/all_to_all | solution.py:113
  81.4 21.5 %all-to-all-done = bf16[16,2,18432]{2,1,0:T(2,128)(2,1)S(1)} async-done(((bf16[16,2,18432]{2,1,0:T(2,128)(2,1)}), bf16[16,2,18432]{2,1,0:T(2,128)(2,1)S(1)}, u32[]{:S(2)}, u32[]{:S(2)}) %all-to-all-start) | async-done | bytes 1179680 | tf_op jit(solution)/shard_map/all_to_all | solution.py:113
  104.5 5.4 %copy.128 = f32[1,4,64,16,144]{4,2,3,1,0:T(8,128)} copy(bf16[1,4,64,16,144]{2,1,4,3,0:T(4,128)(2,1)S(1)} %bitcast.138) | data formatting | bytes 3538944 | tf_op jit(solution)/shard_map/convert_element_type | solution.py:116
  109.8 7.8 %copy_multiply_fusion = f32[1,4,64,16,144]{4,0,3,2,1:T(1,128)S(1)} fusion(f32[1,4,64,16,144]{4,3,2,1,0:T(8,128)} %bitcast.135, f32[64,16]{1,0:T(8,128)S(1)} %copy-done.29), kind=kLoop, calls=%fused_computation.17 | loop fusion | flops 589824 | bytes 4722688 | tf_op jit(solution)/shard_map/mul | solution.py:73
  117.7 5.5 %slice.492 = f32[1,4,64,15,144]{4,0,3,2,1:T(1,128)} slice(f32[1,4,64,16,144]{4,0,3,2,1:T(1,128)S(1)} %copy_multiply_fusion), slice={[0:1], [0:4], [0:64], [0:15], [0:144]} | slice | bytes 4423680 | tf_op jit(solution)/shard_map/slice | solution.py:36
  123.1 5.2 slice.493
  154.5 43.8 %multiply_add_fusion.3 = f32[1,4,64,16,144]{4,0,3,2,1:T(1,128)S(1)} fusion(f32[1,4,64,1,144]{4,0,3,2,1:T(1,128)S(1)} %slice.506, f32[1,4,64,2,144]{4,0,3,2,1:T(1,128)S(1)} %slice.505, f32[1,4,64,3,144]{4,0,3,2,1:T(1,128)S(1)} %slice.504, f32[1,4,64,4,144]{4,0,3,2,1:T(1,128)S(1)} %slice.503, f32[1,4,64,5,144]{4,0,3,2,1:T(1,128)} %slice.502, ...), kind=kLoop, calls=%fused_computation.21 | loop fusion | flops 18284544 | bytes 22426048 | tf_op jit(solution)/shard_map/add | solution.py:35
  235.9 8.1 %copy.152 = f32[1,4,64,15,144]{4,0,3,2,1:T(1,128)} copy(f32[1,4,64,15,144]{4,3,2,1,0:T(8,128)} %slice.526) | data formatting | bytes 4423680
  244.0 8.1 %copy.151 = f32[1,4,64,14,144]{4,0,3,2,1:T(1,128)} copy(f32[1,4,64,14,144]{4,3,2,1,0:T(8,128)} %slice.527) | data formatting | bytes 4128768
  252.2 5.4 %copy.150 = f32[1,4,64,13,144]{4,0,3,2,1:T(1,128)} copy(f32[1,4,64,13,144]{4,3,2,1,0:T(8,128)S(1)} %copy-done.10) | data formatting | bytes 3833856
  273.2 4.8 copy.144
  288.4 35.6 %multiply_add_fusion.1 = f32[1,4,64,16,144]{4,0,3,2,1:T(1,128)S(1)} fusion(f32[1,4,64,2,144]{4,0,3,2,1:T(1,128)S(1)} %copy.139, f32[1,4,64,3,144]{4,0,3,2,1:T(1,128)S(1)} %copy.140, f32[1,4,64,4,144]{4,0,3,2,1:T(1,128)S(1)} %copy.141, f32[1,4,64,5,144]{4,0,3,2,1:T(1,128)S(1)} %copy.142, f32[1,4,64,6,144]{4,0,3,2,1:T(1,128)} %copy.143, ...), kind=kLoop, calls=%fused_computation.19 | loop fusion | flops 16515072 | bytes 22273920 | tf_op jit(solution)/shard_map/add | solution.py:38
  331.0 10.6 %pad.124 = f32[1,4,16,144]{3,0,2,1:T(1,128)S(1)} pad(f32[1,4,8,144]{3,0,2,1:T(1,128)} %pad_maximum_fusion.5, f32[]{:T(128)} %constant.31.clone.1), padding=0_0_0x0_0_0x0_1_1x0_0_0 | pad | bytes 55300 | tf_op jit(solution)/shard_map/pad | solution.py:47
  349.5 9.2 %multiply_add_fusion.2 = f32[1,4,64,16,144]{4,0,3,2,1:T(1,128)} fusion(f32[1,4,64,16,144]{4,0,3,2,1:T(1,128)} %copy-done.6, f32[4,64,144]{2,1,0:T(8,128)S(1)} %pad_bitcast_fusion.1, f32[16,144]{1,0:T(8,128)S(1)} %copy-done.31), kind=kLoop, calls=%fused_computation.20 | loop fusion | flops 1179648 | bytes 4875264 | tf_op jit(solution)/shard_map/add | solution.py:54
  369.5 7.0 %copy.130 = f32[1,4,64,16,144]{4,2,3,1,0:T(8,128)} copy(f32[1,4,64,16,144]{2,1,4,3,0:T(4,128)} %bitcast.139) | data formatting | bytes 4718592 | tf_op jit(solution)/shard_map/mul | solution.py:74
  383.1 54.8 %all_to_all.14 = bf16[16,1,4,64,144]{4,3,2,1,0:T(8,128)(2,1)S(1)} all-to-all(bf16[16,1,4,64,144]{4,3,2,1,0:T(8,128)(2,1)S(1)} %fusion.37), channel_id=1, replica_groups=mesh['orb'=2,'grid'=16] {'grid'}, dimensions={0} | all-to-all | bytes 2359296 | tf_op jit(solution)/shard_map/all_to_all | solution.py:120
  443.3 35.6 %all-gather.2.cloned.1.call-done = bf16[2,4,64,2304]{3,2,1,0:T(8,128)(2,1)} async-done(((bf16[1,4,64,2304]{3,2,1,0:T(8,128)(2,1)}), bf16[2,4,64,2304]{3,2,1,0:T(8,128)(2,1)}) %all-gather.2.cloned.1.call-update) | async-done | bytes 2359312 | tf_op jit(solution)/shard_map/all_gather | solution.py:128
  479.0 6.7 %fusion.30 = bf16[4,64,1280]{2,1,0:T(8,128)(2,1)S(1)} fusion(bf16[2,4,64,2304]{3,2,1,0:T(8,128)(2,1)} %all-gather.2.cloned.1.call-done, bf16[1280,2304]{1,0:T(8,128)(2,1)} %param.7, f32[2,64,1280]{2,1,0:T(8,128)S(1)} %copy-done.27), kind=kOutput, calls=%fused_computation.30 | convolution fusion | flops 3020881920 | bytes 9568256 | tf_op jit(solution)/shard_map/al,ikrl->ikra/dot_general | solution.py:125
  485.7 6.0 %fusion.8 = f32[2304,4,64]{0,2,1:T(8,128)} fusion(bf16[1280,2304]{1,0:T(8,128)(2,1)} %param.7, f32[1280]{0:T(1024)S(1)} %copy-done.75, bf16[4,64,1280]{2,1,0:T(8,128)(2,1)S(1)} %fusion.30), kind=kOutput, calls=%fused_computation.9 | convolution fusion | flops 1518796800 | bytes 8918016 | tf_op jit(solution)/shard_map/al,kra->lkr/dot_general | solution.py:134
  491.7 34.9 %reduce-scatter.5.cloned.1.call-done = f32[1152,4,64]{0,2,1:T(8,128)} async-done(((f32[2304,4,64]{0,2,1:T(8,128)}), f32[1152,4,64]{0,2,1:T(8,128)}) %reduce-scatter.5.cloned.1.call-update) | async-done | bytes 1179664 | tf_op jit(solution)/shard_map/reduce_scatter | solution.py:133
  (324 shorter events, 141.7 us)
Async XLA Ops:
  6.5 15.8 %copy-start = (bf16[4,64,2304]{2,1,0:T(8,128)(2,1)S(1)}, bf16[4,64,2304]{2,1,0:T(8,128)(2,1)}, u32[]{:S(2)}) copy-start(bf16[4,64,2304]{2,1,0:T(8,128)(2,1)} %param.6) | copy-start | bytes 3538948
  6.5 59.0 %reduce-scatter.3.cloned.1.call-start = ((), (), s32[]{:S(2)}) async-start(), calls=%async_computation.4 | async-start | bytes 3538944 | tf_op jit(solution)/shard_map/reduce_scatter | solution.py:100
  6.5 15.8 %slice-start.1 = ((s8[5898240]{0:T(1024)(128)(4,1)}), s8[4194304]{0:T(1024)(128)(4,1)S(1)}, s32[]{:S(2)}) async-start(s8[5898240]{0:T(1024)(128)(4,1)} %bitcast.141), calls=%async_computation.8 | async-start | bytes 8388608
  72.2 30.8 %all-to-all-start = ((bf16[16,2,18432]{2,1,0:T(2,128)(2,1)}), bf16[16,2,18432]{2,1,0:T(2,128)(2,1)S(1)}, u32[]{:S(2)}, u32[]{:S(2)}) async-start(bf16[16,2,18432]{2,1,0:T(2,128)(2,1)} %reshape.327), calls=%async_computation.1 | async-start | bytes 2359296 | tf_op jit(solution)/shard_map/all_to_all | solution.py:113
  77.8 401.2 %all-gather.2.cloned.1.call-start = ((), (), s32[]{:S(2)}) async-start(), calls=%async_computation.5 | async-start | bytes 3538944 | tf_op jit(solution)/shard_map/all_gather | solution.py:128
  154.4 46.2 %copy-start.32 = (f32[144]{0:T(256)S(1)}, f32[144]{0:T(256)}, u32[]{:S(2)}) copy-start(f32[144]{0:T(256)} %get-tuple-element.42) | copy-start | bytes 1732
  154.4 46.3 %copy-start.68 = (f32[144]{0:T(256)S(1)}, f32[144]{0:T(256)}, u32[]{:S(2)}) copy-start(f32[144]{0:T(256)} %get-tuple-element.43) | copy-start | bytes 1732
  154.4 46.4 %copy-start.69 = (f32[144]{0:T(256)S(1)}, f32[144]{0:T(256)}, u32[]{:S(2)}) copy-start(f32[144]{0:T(256)} %get-tuple-element.47) | copy-start | bytes 1732
  154.4 46.5 %copy-start.70 = (f32[144]{0:T(256)S(1)}, f32[144]{0:T(256)}, u32[]{:S(2)}) copy-start(f32[144]{0:T(256)} %get-tuple-element.46) | copy-start | bytes 1732
  154.4 46.5 %copy-start.71 = (f32[144]{0:T(256)S(1)}, f32[144]{0:T(256)}, u32[]{:S(2)}) copy-start(f32[144]{0:T(256)} %get-tuple-element.44) | copy-start | bytes 1732
  154.4 46.5 %copy-start.73 = (f32[144]{0:T(256)S(1)}, f32[144]{0:T(256)}, u32[]{:S(2)}) copy-start(f32[144]{0:T(256)} %get-tuple-element.45) | copy-start | bytes 1732
  208.7 26.2 %copy-start.2 = (f32[1,4,64,16,144]{4,3,2,1,0:T(8,128)}, f32[1,4,64,16,144]{4,3,2,1,0:T(8,128)S(1)}, u32[]{:S(2)}) copy-start(f32[1,4,64,16,144]{4,3,2,1,0:T(8,128)S(1)} %broadcast_multiply_fusion.1) | copy-start | bytes 7077892
  271.0 17.1 %copy-start.19 = (f32[1,4,64,11,144]{4,0,3,2,1:T(1,128)S(1)}, f32[1,4,64,11,144]{4,0,3,2,1:T(1,128)}, u32[]{:S(2)}) copy-start(f32[1,4,64,11,144]{4,0,3,2,1:T(1,128)} %copy.148) | copy-start | bytes 4866052
  273.2 14.4 %copy-start.23 = (f32[1,4,64,2,144]{4,3,2,1,0:T(2,128)S(1)}, f32[1,4,64,2,144]{4,3,2,1,0:T(2,128)}, u32[]{:S(2)}) copy-start(f32[1,4,64,2,144]{4,3,2,1,0:T(2,128)} %slice.539) | copy-start | bytes 884740
  273.2 15.0 %copy-start.18 = (f32[1,4,64,13,144]{4,0,3,2,1:T(1,128)S(1)}, f32[1,4,64,13,144]{4,0,3,2,1:T(1,128)}, u32[]{:S(2)}) copy-start(f32[1,4,64,13,144]{4,0,3,2,1:T(1,128)} %copy.150) | copy-start | bytes 5750788
  288.4 35.6 %copy-start.22 = (f32[1,4,64,1,144]{4,3,2,1,0:T(1,128)S(1)}, f32[1,4,64,1,144]{4,3,2,1,0:T(1,128)}, u32[]{:S(2)}) copy-start(f32[1,4,64,1,144]{4,3,2,1,0:T(1,128)} %slice.540) | copy-start | bytes 442372
  288.4 35.6 %copy-start.36 = (f32[144]{0:T(256)S(1)}, f32[144]{0:T(256)}, u32[]{:S(2)}) copy-start(f32[144]{0:T(256)} %get-tuple-element.41) | copy-start | bytes 1732
  326.3 19.3 %copy-start.24 = (f32[1,4,64,144]{3,0,2,1:T(1,128)}, f32[1,4,64,144]{3,0,2,1:T(1,128)S(1)}, u32[]{:S(2)}) copy-start(f32[1,4,64,144]{3,0,2,1:T(1,128)S(1)} %slice_bitcast_fusion) | copy-start | bytes 442372
  329.6 17.6 %slice-start.4 = ((f32[1,4,64,144]{3,0,2,1:T(1,128)}), f32[1,4,1,144]{3,0,2,1:T(1,128)S(1)}, s32[]{:S(2)}) async-start(f32[1,4,64,144]{3,0,2,1:T(1,128)} %copy-done.25), calls=%async_computation.11 | async-start | bytes 8192 | tf_op jit(solution)/shard_map/slice | solution.py:44
  329.6 17.6 %copy-start.28 = (f32[1,4,31,144]{3,0,2,1:T(1,128)S(1)}, f32[1,4,31,144]{3,0,2,1:T(1,128)}, u32[]{:S(2)}) copy-start(f32[1,4,31,144]{3,0,2,1:T(1,128)} %fusion.54) | copy-start | bytes 214276
  437.9 41.0 %copy-start.27 = (f32[2,64,1280]{2,1,0:T(8,128)S(1)}, f32[2,64,1280]{2,1,0:T(8,128)}, u32[]{:S(2)}) copy-start(f32[2,64,1280]{2,1,0:T(8,128)} %copy-done.26) | copy-start | bytes 1966084
  443.3 42.4 %copy-start.75 = (f32[1280]{0:T(1024)S(1)}, f32[1280]{0:T(1024)}, u32[]{:S(2)}) copy-start(f32[1280]{0:T(1024)} %param.8) | copy-start | bytes 15364
  443.3 83.3 %reduce-scatter.5.cloned.1.call-start = ((), (), s32[]{:S(2)}) async-start(), calls=%async_computation.6 | async-start | bytes 3538944 | tf_op jit(solution)/shard_map/reduce_scatter | solution.py:133
  485.7 43.3 %copy-start.1 = (bf16[4,64,2304]{2,1,0:T(8,128)(2,1)S(1)}, bf16[4,64,2304]{2,1,0:T(8,128)(2,1)}, u32[]{:S(2)}) copy-start(bf16[4,64,2304]{2,1,0:T(8,128)(2,1)} %param.6) | copy-start | bytes 3538948
  (61 other events, 344.4 us)
Sparse Core Ops, SparseCore 0:
  29.3 36.1 reduce-scatter.2
  443.4 35.5 all-gather.1
  491.8 34.6 reduce-scatter.4
